TPU v7x, 256 devices: a whole 4x4x8 slice. The times are simulated.
256 devices in a mesh: gx: 8 (over z), gy: 32 (over y, x, core).
Axes of the slice: x: 4, y: 4, z: 8, core: 2. Of those that a mesh axis runs over, the one named last changes fastest.
Arguments:
- queries: bfloat16 [4096, 4096], P('gy', 'gx'), may hold values from -8 to 8
- new_kv: bfloat16 [4096, 8, 128], P('gy', 'gx'), may hold values from -8 to 8
- kv_cache: bfloat16 [16384, 8, 128], P('gy', 'gx'), may hold values from -8 to 8
- cache_seg: int32 [16384], P('gy'), may hold values from -1 to 15, as said below
- cache_slot: int32 [4096], P('gy'), may hold values from 0 to 16383, as said below
- token_seg: int32 [4096], P('gy'), may hold values from 0 to 15, never falling along the last dimension, each value on 1 to 2048 neighbouring positions
- pad_mask: int32 [4096], P('gy'), may hold values 0 or 1
- sink_logits: float32 [64], P('gx'), may hold values from 0 to 4
- out_weight: bfloat16 [4096, 2880], P('gx', 'gy'), may hold values from -0.75 to 0.75
- out_bias: float32 [2880], P('gx'), may hold values from -2 to 2
Outputs:
- attended: bfloat16 [4096, 2880], P('gy', 'gx')
- cache_out: bfloat16 [16384, 8, 128], P('gy', 'gx')
Inputs may be any that keep to these rules, and one draw needn't show every extreme that they name: `cache_seg`: the sequence whose cached key and value a slot holds, or -1 for an empty slot. Distinct slots, each empty (-1) in cache_seg; cache_slot[t] // 512 == t // 128.
All inputs are finite; a program needn't handle non-finite values. No bound on the sum of `pad_mask` on one device may be relied on, other than what follows from the above.
Results may differ from a plain program's by a relative error of at most 0.015.
Values may be sent and summed in bfloat16 or wider, within the bound.
A program may use at most 128 MiB of HBM per device.

v0:
```python
import math

import jax
import jax.numpy as jnp
from jax import lax
from jax.sharding import PartitionSpec as P


def shards(
    queries,
    new_kv,
    kv_cache,
    cache_seg,
    cache_slot,
    token_seg,
    pad_mask,
    sink_logits,
    out_weight,
    out_bias,
):
    local_tokens = queries.shape[0]
    local_slots = kv_cache.shape[0]
    local_groups = kv_cache.shape[1]
    head_dim = kv_cache.shape[2] // 2
    group_heads = queries.shape[1] // (local_groups * head_dim)
    scale = head_dim ** (-0.5)
    own_index = lax.axis_index("gy")
    first_token = own_index * local_tokens
    live_rows = pad_mask == 1
    target = jnp.where(live_rows, cache_slot - own_index * local_slots, local_slots)
    cache_out = kv_cache.at[target].set(new_kv, mode="drop")
    token_index = first_token + jnp.arange(local_tokens, dtype=jnp.int32)
    slot_seg = cache_seg.at[target].set(token_seg, mode="drop")
    slot_order = jnp.full((local_slots,), -1, jnp.int32).at[target].set(token_index, mode="drop")
    sink_table = sink_logits.reshape(local_groups, group_heads)
    query_heads = queries.reshape(local_tokens, local_groups, group_heads, head_dim)
    initial = (
        jnp.broadcast_to(sink_table[:, :, None], (local_groups, group_heads, local_tokens)),
        jnp.ones((local_groups, group_heads, local_tokens), jnp.float32),
        jnp.zeros((local_groups, group_heads, local_tokens, head_dim), jnp.float32),
    )
    kv_rows = lax.all_gather(cache_out, "gy", axis=0, tiled=True)
    seg_rows = lax.all_gather(slot_seg, "gy", axis=0, tiled=True)
    order_rows = lax.all_gather(slot_order, "gy", axis=0, tiled=True)
    total_rows = kv_rows.shape[0]
    blk_rows = math.gcd(total_rows, 512)
    count_blocks = total_rows // blk_rows
    stacked = (
        kv_rows.reshape(count_blocks, blk_rows, local_groups, 2 * head_dim),
        seg_rows.reshape(count_blocks, blk_rows),
        order_rows.reshape(count_blocks, blk_rows),
    )

    def one_block(running, block_data):
        run_peak, weight_sum, weighted = running
        block_kv, block_seg, block_order = block_data
        visible = (block_seg[None, :] == token_seg[:, None]) & (
            block_order[None, :] <= token_index[:, None]
        )
        scores = (
            jnp.einsum(
                "tgqd,cgd->gqtc",
                query_heads,
                block_kv[:, :, :head_dim],
                preferred_element_type=jnp.float32,
            )
            * scale
        )
        new_peak = jnp.maximum(run_peak, jnp.max(jnp.where(visible, scores, -jnp.inf), axis=-1))
        rescale = jnp.exp(run_peak - new_peak)
        weights = jnp.where(visible, jnp.exp(scores - new_peak[..., None]), 0.0)
        weight_sum = weight_sum * rescale + jnp.sum(weights, axis=-1)
        weighted = weighted * rescale[..., None] + jnp.einsum(
            "gqtc,cgd->gqtd",
            weights.astype(jnp.bfloat16),
            block_kv[:, :, head_dim:],
            preferred_element_type=jnp.float32,
        )
        return ((new_peak, weight_sum, weighted), None)

    result, unused = lax.scan(one_block, initial, stacked)
    run_peak, weight_sum, weighted = result
    attn_heads = jnp.transpose(weighted / weight_sum[..., None], (2, 0, 1, 3)).reshape(
        local_tokens, local_groups * group_heads * head_dim
    )
    attention = (attn_heads * pad_mask[:, None].astype(jnp.float32)).astype(jnp.bfloat16)
    partial_out = jnp.dot(
        attention,
        lax.all_gather(out_weight, "gy", axis=1, tiled=True),
        preferred_element_type=jnp.float32,
    )
    summed = lax.psum_scatter(
        partial_out.astype(jnp.bfloat16), "gx", scatter_dimension=1, tiled=True
    ).astype(jnp.float32)
    return ((summed + out_bias).astype(jnp.bfloat16), cache_out)


def solution(mesh):
    placed = (
        P("gy", "gx"),
        P("gy", "gx", None),
        P("gy", "gx", None),
        P("gy"),
        P("gy"),
        P("gy"),
        P("gy"),
        P("gx"),
        P("gx", "gy"),
        P("gx"),
    )
    return jax.shard_map(
        shards,
        mesh=mesh,
        in_specs=placed,
        out_specs=(P("gy", "gx"), P("gy", "gx", None)),
        check_vma=False,
    )
```

profile of v0, /device:TPU:4, one launch (start us, length us, event | category | flops | bytes accessed | tf_op | source)
XLA Modules:
  0.0 257.3 jit_solution(15577354305980435805)
XLA Ops:
  7.2 0.9 copy.47
  9.7 1.0 scatter_custom_fusion.2
  11.4 1.0 scatter_custom_fusion.1
  12.4 24.2 %all-gather.2 = s32[32,1,512]{2,1,0:T(1,128)S(1)} all-gather(s32[1,1,512]{2,1,0:T(1,128)S(1)} %bitcast.122), channel_id=1, replica_groups=mesh['gx'=8,'gy'=32] {'gy'}, dimensions={0}, use_global_device_ids=true | all-gather | bytes 67584 | tf_op jit(solution)/shard_map/all_gather | solution.py:44
  36.6 1.1 scatter_fusion
  37.7 22.4 %all-gather.1 = s32[32,1,512]{2,1,0:T(1,128)S(1)} all-gather(s32[1,1,512]{2,1,0:T(1,128)S(1)} %bitcast.107), channel_id=1, replica_groups=mesh['gx'=8,'gy'=32] {'gy'}, dimensions={0}, use_global_device_ids=true | all-gather | bytes 67584 | tf_op jit(solution)/shard_map/all_gather | solution.py:43
  60.3 2.5 all-gather.9.cloned.1.call-done
  62.8 4.4 %reshape.95 = bf16[2880,512]{1,0:T(8,128)(2,1)} reshape(bf16[32,90,512]{2,1,0:T(8,128)(2,1)} %all-gather.9.cloned.1.call-done) | data formatting | bytes 5898240
  67.2 49.0 %all-gather.7.cloned.1.call-done = bf16[16384,128]{1,0:T(8,128)(2,1)} async-done(((bf16[512,128]{1,0:T(8,128)(2,1)}), bf16[16384,128]{1,0:T(8,128)(2,1)}) %all-gather.7.cloned.1.call-update) | async-done | bytes 4194320 | tf_op jit(solution)/shard_map/all_gather | solution.py:42
  116.3 90.2 %while.15 = (s32[]{:T(128)}, f32[1,8,128]{2,1,0:T(8,128)S(1)}, f32[1,8,128]{2,1,0:T(8,128)S(1)}, f32[1,8,128,64]{2,3,1,0:T(8,128)S(1)}, s32[32,512]{1,0:T(8,128)...) while((s32[]{:T(128)}, f32[1,8,128]{2,1,0:T(8,128)S(1)}, ...), condition=%wide.region_6.7_spmd.clone, body=%wide.region_3.6_spmd.clone.sunk | while | flops 140382336 | bytes 7943820 | solution.py:81
  116.5 0.9 constant_dynamic-slice_fusion.6
  119.3 0.9 constant_dynamic-slice_fusion.6
  122.1 0.9 constant_dynamic-slice_fusion.6
  124.9 0.9 constant_dynamic-slice_fusion.6
  127.8 0.9 constant_dynamic-slice_fusion.6
  130.6 0.9 constant_dynamic-slice_fusion.6
  133.4 0.9 constant_dynamic-slice_fusion.6
  136.2 0.9 constant_dynamic-slice_fusion.6
  139.1 0.9 constant_dynamic-slice_fusion.6
  141.9 0.9 constant_dynamic-slice_fusion.6
  144.7 0.9 constant_dynamic-slice_fusion.6
  206.6 3.6 %convolution_convert_fusion = bf16[128,2880]{0,1:T(8,128)(2,1)} fusion(bf16[2880,512]{1,0:T(8,128)(2,1)} %reshape.95, bf16[128,512]{0,1:T(8,128)(2,1)S(1)} %fusion.19), kind=kOutput, calls=%fused_computation.35 | convolution fusion | flops 377856000 | bytes 3817472 | tf_op jit(solution)/shard_map/dot_general | solution.py:87
  210.3 38.9 %reduce-scatter.4.cloned.1.call-done = bf16[128,360]{0,1:T(8,128)(2,1)} async-done(((bf16[128,2880]{0,1:T(8,128)(2,1)}), bf16[128,360]{0,1:T(8,128)(2,1)}) %reduce-scatter.4.cloned.1.call-update) | async-done | bytes 92176
  249.1 1.6 add_convert_fusion
  (369 shorter events, 79.6 us)
Async XLA Ops:
  7.2 2.5 copy-start
  7.2 53.0 %copy-start.2 = (bf16[128,512]{1,0:T(8,128)(2,1)S(1)}, bf16[128,512]{1,0:T(8,128)(2,1)}, u32[]{:S(2)}) copy-start(bf16[128,512]{1,0:T(8,128)(2,1)} %param.12) | copy-start | bytes 393220
  7.2 55.6 %all-gather.9.cloned.1.call-start = ((), (), s32[]{:S(2)}) async-start(), calls=%async_computation.2 | async-start | bytes 3244032 | tf_op jit(solution)/shard_map/all_gather | solution.py:89
  8.9 107.3 %all-gather.7.cloned.1.call-start = ((), (), s32[]{:S(2)}) async-start(), calls=%async_computation.1 | async-start | bytes 4325376 | tf_op jit(solution)/shard_map/all_gather | solution.py:42
  10.7 0.7 copy-start.1
  11.4 237.8 %reduce-scatter.4.cloned.1.call-start = ((), (), s32[]{:S(2)}) async-start(), calls=%async_computation.3 | async-start | bytes 829440
  60.3 55.9 %copy-start.5 = (f32[8]{0:T(128)S(1)}, f32[8]{0:T(128)}, u32[]{:S(2)}) copy-start(f32[8]{0:T(128)} %param.19) | copy-start | bytes 100
  60.3 56.0 %copy-start.3 = (s32[128]{0:T(128)S(1)}, s32[128]{0:T(128)}, u32[]{:S(2)}) copy-start(s32[128]{0:T(128)} %param.17) | copy-start | bytes 1540
  206.6 42.5 %copy-start.4 = (f32[360]{0:T(512)S(1)}, f32[360]{0:T(512)}, u32[]{:S(2)}) copy-start(f32[360]{0:T(512)} %param.21) | copy-start | bytes 4324
Sparse Core Ops, SparseCore 0:
  10.5 52.1 all-gather.8
  65.9 50.2 all-gather.6
  210.4 38.6 reduce-scatter.3
where the time goes:
time: 258 us; the launch traced here: 257 us
  waiting for transfers between devices  90.3 us (35%)
  blocking collectives  46.6 us (18%)
  local copies, waits for them, and re-layouts  43.6 us (17%)
  matrix products  36 us (14%)
  other arithmetic  23.7 us (9%)
  between operations  13.9 us (5%)
  loops' own time  3.05 us (1%)
    all_gather x1, waiting for transfers between devices, shards(): kv_rows = lax.all_gather(cache_out, 'gy', axis=0, tiled=True)  49 us
    unnamed x4, waiting for transfers between devices  38.9 us
    dynamic_slice x96, local copies, waits for them, and re-layouts, shards(): result, unused = lax.scan(one_block, initial, stacked)  33.5 us
    all_gather x1, blocking collectives, shards(): order_rows = lax.all_gather(slot_order, 'gy', axis=0, tiled=True)  24.2 us
    all_gather x1, blocking collectives, shards(): seg_rows = lax.all_gather(slot_seg, 'gy', axis=0, tiled=True)  22.4 us
    dot_general x32, matrix products, one_block(): jnp.einsum('gqtc,cgd->gqtd', weights.astype(jnp.bfloat16), block_kv[:, :,...  17.4 us
    dot_general x32, matrix products, one_block(): jnp.einsum('tgqd,cgd->gqtc', query_heads, block_kv[:, :, :head_dim], pref...  15 us
    reduce_sum x32, other arithmetic, one_block(): weight_sum = weight_sum * rescale + jnp.sum(weights, axis=-1)  14 us
  transfers between devices with their start and end apart: 3, of which 3 were waited for; matrix products, arithmetic and copies ran while one was open for 3% of the time, Pallas kernels for 0%

commit v1 on v0

v1 whole, which is shorter than its diff:
```python
import jax
import jax.numpy as jnp
from jax import lax
from jax.experimental import pallas as pl
from jax.experimental.pallas import tpu as pltpu
from jax.sharding import PartitionSpec as P

MESH = pl.DeviceIdType.MESH
F32 = jnp.float32
BF16 = jnp.bfloat16
NX, NY, NC = 4, 4, 2
NBLK = NX * NY * NC
SLOTS = 512
TOK = 128
META = 16
KVROWS = SLOTS + META
WCOLS = 90
WPAD = 96
WROWS = 4 * WPAD
ROWS = KVROWS + WROWS
PENALTY = -1048576.0
VMEM_LIMIT = 60 * 1024 * 1024
NT = (((1,), (1,)), ((), ()))


def iota(shape, axis):
    return lax.broadcasted_iota(jnp.int32, shape, axis)


def to_column(row):
    return jnp.transpose(jnp.broadcast_to(row, (8, row.shape[1])))[:, :1]


def prep_kernel(new_ref, kv_ref, cseg_ref, cslot_ref, tseg_ref, pad_ref, wt_ref, cache_ref, blk_ref, own_ref):
    own = lax.axis_index("gy")
    target = jnp.where(pad_ref[...] == 1, cslot_ref[...] - own * SLOTS, SLOTS)
    target_f = target.astype(F32)
    tseg_f = tseg_ref[...].astype(F32)
    place = (iota((SLOTS, TOK), 0).astype(F32) == target_f).astype(F32)
    place_b = place.astype(BF16)
    hit_col = jnp.sum(place, axis=1, keepdims=True)
    put = jnp.dot(place_b, new_ref[...], preferred_element_type=F32)
    cache = jnp.where(hit_col > 0.5, put, kv_ref[...].astype(F32)).astype(BF16)
    cache_ref[...] = cache
    order = iota((1, TOK), 1).astype(F32) + 1.0
    which = iota((8, TOK), 0)
    facts = jnp.where(which == 0, tseg_f, jnp.where(which == 1, order, jnp.where(which == 2, 1.0, 0.0)))
    spread = lax.dot_general(facts.astype(BF16), place_b, NT, preferred_element_type=F32)
    hit = spread[2:3] > 0.5
    cseg_f = cseg_ref[...].astype(F32)
    key = jnp.where(hit, spread[0:1], jnp.where(cseg_f < 0.0, 16.0, cseg_f))
    ordered = spread[1:2]
    which = iota((8, SLOTS), 0)
    own_ref[...] = jnp.where(which == 0, key, jnp.where(which == 1, ordered, 0.0))
    double = key * 2.0 + jnp.where(hit, 1.0, 0.0)
    unique = double * SLOTS + iota((1, SLOTS), 1).astype(F32)
    unique_col = to_column(unique)
    rank = jnp.sum((unique_col < unique).astype(F32), axis=0, keepdims=True)
    permute = (iota((SLOTS, SLOTS), 0).astype(F32) == rank).astype(BF16)
    blk_ref[:SLOTS, :] = jnp.dot(permute, cache, preferred_element_type=F32).astype(BF16)
    double_col = to_column(double)
    lane_seg = ((iota((1, 128), 1) - 64) * 2).astype(F32)
    start = jnp.sum((double_col < lane_seg).astype(F32), axis=0, keepdims=True)
    middle = jnp.sum((double_col < lane_seg + 1.0).astype(F32), axis=0, keepdims=True)
    end = jnp.sum((double_col < lane_seg + 2.0).astype(F32), axis=0, keepdims=True)
    rows = []
    for value in (start, middle, end):
        high = jnp.where(value >= 512.0, 2.0, jnp.where(value >= 256.0, 1.0, 0.0))
        rows += [value - 256.0 * high, high]
    which = iota((META, 128), 0)
    meta = jnp.zeros((META, 128), F32)
    for i, row in enumerate(rows):
        meta = jnp.where(which == i, row, meta)
    blk_ref[SLOTS:KVROWS, :] = meta.astype(BF16)
    weights = jnp.concatenate([wt_ref[...].astype(F32), jnp.zeros((WPAD - WCOLS, 4 * 128), F32)], axis=0)
    for k in range(4):
        blk_ref[KVROWS + k * WPAD : KVROWS + (k + 1) * WPAD, :] = weights[:, k * 128 : (k + 1) * 128].astype(BF16)


def splits(rows):
    units = rows // 16
    edges = [0]
    for i in range(4):
        edges.append(edges[-1] + 16 * ((units + 3 - i) // 4))
    return edges


def gather_kernel(copies, blk_ref, out_ref, local_sem, send_sem, recv_sem):
    gx = lax.axis_index("gx")
    gy = lax.axis_index("gy")
    core = gy % NC
    x = (gy // NC) % NX
    y = gy // (NC * NX)

    def index(xx, yy, cc):
        return ((yy % NY) * NX + xx % NX) * NC + cc

    xp, xm = index(x + 1, y, core), index(x + 3, y, core)
    yp, ym = index(x, y + 1, core), index(x, y + 3, core)
    mate = index(x, y, 1 - core)
    barrier = pltpu.get_barrier_semaphore()
    for peer in (xp, xm, yp, ym, mate):
        pl.semaphore_signal(barrier, inc=1, device_id=(gx, peer), device_id_type=MESH)
    own = index(x, y, core)
    local = pltpu.make_async_copy(blk_ref, out_ref.at[own], local_sem)
    local.start()
    pl.semaphore_wait(barrier, 5)
    edges = splits(blk_ref.shape[0])
    used = [0]
    started = []
    mates = []

    def send(block, lo, hi, peer, fresh=False):
        slot = used[0]
        used[0] += 1
        rows = pl.ds(lo, hi - lo)
        source = blk_ref.at[rows] if fresh else out_ref.at[block, rows]
        copy = pltpu.make_async_remote_copy(
            src_ref=source,
            dst_ref=out_ref.at[block, rows],
            send_sem=send_sem.at[slot],
            recv_sem=recv_sem.at[slot],
            device_id=(gx, peer),
            device_id_type=MESH,
        )
        copy.start()
        started.append(copy)
        if peer is mate:
            mates.append(copy)
        return copy

    halves = []
    for half in range(2):
        lo, mid, hi = edges[2 * half], edges[2 * half + 1], edges[2 * half + 2]
        if half == 0:
            first, second = (xp, xm), (yp, ym)
            place = lambda i, j: index(x + i, y + j, core)
        else:
            first, second = (yp, ym), (xp, xm)
            place = lambda i, j: index(x + j, y + i, core)
        halves.append((lo, mid, hi, first, second, place))

    near = []
    for lo, mid, hi, first, second, place in halves:
        a = send(own, lo, hi, first[0], True)
        b = send(own, lo, hi, first[1], True)
        near.append((a, b))
    far = [[] for _ in halves]
    for h, (lo, mid, hi, first, second, place) in enumerate(halves):
        c = send(own, lo, hi, second[0], True)
        d = send(own, lo, hi, second[1], True)
        far[h].append((0, lo, mid, hi, c, d))
        send(own, lo, hi, mate, True)
    forward = []
    for h, (lo, mid, hi, first, second, place) in enumerate(halves):
        a, b = near[h]
        a.wait_recv()
        fa = send(place(3, 0), lo, mid, first[0])
        c = send(place(3, 0), lo, hi, second[0])
        d = send(place(3, 0), lo, hi, second[1])
        far[h].append((3, lo, mid, hi, c, d))
        b.wait_recv()
        fb = send(place(1, 0), mid, hi, first[1])
        c = send(place(1, 0), lo, hi, second[0])
        d = send(place(1, 0), lo, hi, second[1])
        far[h].append((1, lo, mid, hi, c, d))
        send(place(3, 0), lo, hi, mate)
        send(place(1, 0), lo, hi, mate)
        forward.append((fa, fb))
    last = []

    def relay(h, entry):
        i, lo, mid, hi, c, d = entry
        _, _, _, _, second, place = halves[h]
        c.wait_recv()
        last.append(send(place(i, 3), lo, mid, second[0]))
        d.wait_recv()
        last.append(send(place(i, 1), mid, hi, second[1]))
        send(place(i, 3), lo, hi, mate)
        send(place(i, 1), lo, hi, mate)

    for h in range(2):
        relay(h, far[h][0])
    pieces = []
    for h, (lo, mid, hi, first, second, place) in enumerate(halves):
        fa, fb = forward[h]
        fa.wait_recv()
        c0 = send(place(2, 0), lo, mid, second[0])
        d0 = send(place(2, 0), lo, mid, second[1])
        fb.wait_recv()
        c1 = send(place(2, 0), mid, hi, second[0])
        d1 = send(place(2, 0), mid, hi, second[1])
        send(place(2, 0), lo, hi, mate)
        pieces.append((c0, d0, c1, d1))
    for e in range(1, 3):
        for h in range(2):
            relay(h, far[h][e])
    for h, (lo, mid, hi, first, second, place) in enumerate(halves):
        c0, d0, c1, d1 = pieces[h]
        c0.wait_recv()
        last.append(send(place(2, 3), lo, mid, second[0]))
        d1.wait_recv()
        last.append(send(place(2, 1), mid, hi, second[1]))
        c1.wait_recv()
        send(place(2, 3), lo, hi, mate)
        d0.wait_recv()
        send(place(2, 1), lo, hi, mate)
    order = [(0, 0), (1, 0), (0, 3), (1, 3), (0, 1), (1, 1), (0, 2), (1, 2)]
    for n, (h, i) in enumerate(order):
        lo, mid, hi, first, second, place = halves[h]
        last[2 * n].wait_recv()
        last[2 * n + 1].wait_recv()
        send(place(i, 2), lo, hi, mate)
    for copy in mates:
        copy.wait_recv()
    for copy in started:
        copy.wait_send()
    local.wait()
    assert used[0] == copies


def attend_kernel(
    sink_ref, tseg_s, q_ref, cache_ref, own_ref, tseg_ref, pad_ref, g_ref,
    out_ref, buf, ka, va, qa, m_ref, acc_ref, bound_v, bound_s, lo_ref, hi_ref, sems,
):
    own_block = lax.axis_index("gy")
    load = pltpu.make_async_copy(g_ref.at[:, pl.ds(0, KVROWS)], buf.at[:, pl.ds(0, KVROWS)], sems.at[0])
    load.start()
    lane = iota((1, 128), 1)
    low = lane < 64
    tseg_col = to_column(tseg_ref[...].astype(F32))
    pad_col = to_column(pad_ref[...].astype(F32))
    seg_hot = (tseg_col == (lane - 64).astype(F32)).astype(F32)
    for pair in range(4):
        two = q_ref[:, pair * 128 : (pair + 1) * 128].astype(F32) * 0.125
        qa[2 * pair * TOK : (2 * pair + 1) * TOK, :] = jnp.where(low, two, seg_hot).astype(BF16)
        qa[(2 * pair + 1) * TOK : (2 * pair + 2) * TOK, :] = jnp.where(low, pltpu.roll(two, 64, 1), seg_hot).astype(BF16)
    position = iota((TOK, 1), 0).astype(F32) + 1.0
    shown = (own_ref[0:1, :] == tseg_col) & (own_ref[1:2, :] <= position)
    bias = jnp.where(shown, 0.0, PENALTY)
    kv = cache_ref[...].astype(F32)
    k_own = jnp.where(low, kv, 0.0).astype(BF16)
    v_own = jnp.where(low, 1.0, kv).astype(BF16)
    for h in range(8):
        rows = slice(h * TOK, (h + 1) * TOK)
        scores = lax.dot_general(qa[rows, :], k_own, NT, preferred_element_type=F32) + bias
        peak = jnp.maximum(jnp.max(scores, axis=1, keepdims=True), sink_ref[h])
        weights = jnp.exp(scores - peak)
        acc = jnp.dot(weights.astype(BF16), v_own, preferred_element_type=F32)
        acc_ref[rows, :] = acc + jnp.where(low, jnp.exp(sink_ref[h] - peak), 0.0)
        m_ref[rows, :] = peak
    load.wait()
    seg_lo, seg_hi = tseg_s[0], tseg_s[TOK - 1]
    for b in range(NBLK):
        meta = buf[b, SLOTS:KVROWS, :].astype(F32)
        start = meta[0:1] + 256.0 * meta[1:2]
        middle = meta[2:3] + 256.0 * meta[3:4]
        end = meta[4:5] + 256.0 * meta[5:6]
        lo_ref[b : b + 1, :] = start.astype(jnp.int32)
        hi_ref[b : b + 1, :] = jnp.where(b < own_block, end, middle).astype(jnp.int32)
    lo_all, hi_all = lo_ref[...], hi_ref[...]
    wide = iota((NBLK, 128), 1)
    begin = jnp.sum(jnp.where(wide == seg_lo + 64, lo_all, 0).astype(F32), axis=1, keepdims=True)
    stop = jnp.sum(jnp.where(wide == seg_hi + 64, hi_all, 0).astype(F32), axis=1, keepdims=True)
    bound_v[...] = jnp.where(wide == 0, begin, jnp.where(wide == 1, stop, 0.0)).astype(jnp.int32)
    fetch = pltpu.make_async_copy(bound_v, bound_s, sems.at[1])
    fetch.start()
    fetch.wait()

    def pack_block(b, off):
        first, stop = bound_s[b, 0], bound_s[b, 1]
        base = (first // 16) * 16
        length = jnp.where((b == own_block) | (stop <= first), 0, stop - base)
        low_row = lo_ref[pl.ds(b, 1), :]
        high_row = hi_ref[pl.ds(b, 1), :]

        def piece(i, carry):
            src = pl.multiple_of(base + 64 * i, 16)
            dst = pl.multiple_of(off + 64 * i, 16)
            row = src + iota((64, 128), 0)
            kv = jnp.where(row < SLOTS, buf[b, pl.ds(src, 64), :].astype(F32), 0.0)
            penalty = jnp.where((row >= low_row) & (row < high_row), 0.0, PENALTY)
            ka[pl.ds(dst, 64), :] = jnp.where(low, kv, penalty).astype(BF16)
            va[pl.ds(dst, 64), :] = jnp.where(low, 1.0, kv).astype(BF16)
            return carry

        lax.fori_loop(0, (length + 63) // 64, piece, 0)
        return off + ((length + 15) // 16) * 16

    total = lax.fori_loop(0, NBLK, pack_block, 0)
    tail = pl.multiple_of(total, 16)
    ka[pl.ds(tail, 512), :] = jnp.broadcast_to(jnp.where(low, 0.0, PENALTY), (512, 128)).astype(BF16)
    va[pl.ds(tail, 512), :] = jnp.broadcast_to(jnp.where(low, 1.0, 0.0), (512, 128)).astype(BF16)

    def chunk(i, carry):
        at = pl.multiple_of(i * 512, 512)
        keys, values = ka[pl.ds(at, 512), :], va[pl.ds(at, 512), :]
        for r in range(4):
            rows = slice(r * 256, (r + 1) * 256)
            scores = lax.dot_general(qa[rows, :], keys, NT, preferred_element_type=F32)
            old = m_ref[rows, :]
            peak = jnp.maximum(old, jnp.max(scores, axis=1, keepdims=True))
            weights = jnp.exp(scores - peak)
            acc = jnp.dot(weights.astype(BF16), values, preferred_element_type=F32)
            acc_ref[rows, :] = acc_ref[rows, :] * jnp.exp(old - peak) + acc
            m_ref[rows, :] = peak
        return carry

    lax.fori_loop(0, (total + 511) // 512, chunk, 0)
    for pair in range(4):
        even = acc_ref[2 * pair * TOK : (2 * pair + 1) * TOK, :]
        odd = acc_ref[(2 * pair + 1) * TOK : (2 * pair + 2) * TOK, :]
        top = jnp.where(low, pltpu.roll(even, 64, 1), odd)
        bottom = jnp.where(low, even, pltpu.roll(odd, 64, 1))
        out_ref[:, pair * 128 : (pair + 1) * 128] = (top / bottom * pad_col).astype(BF16)


def project_kernel(nz, attn_ref, bias_ref, g_ref, out_ref, wbuf, sbuf, rbuf, load_sem, send_sem, recv_sem):
    gx = lax.axis_index("gx")
    gy = lax.axis_index("gy")
    load = pltpu.make_async_copy(g_ref.at[:, pl.ds(KVROWS, WROWS)], wbuf, load_sem)
    load.start()
    barrier = pltpu.get_barrier_semaphore()
    for d in range(1, nz):
        pl.semaphore_signal(barrier, inc=1, device_id=((gx + d) % nz, gy), device_id_type=MESH)
    load.wait()

    def partial(dest):
        parts = []
        for b in range(4):
            total = jnp.zeros((WPAD, TOK), F32)
            for k in range(4):
                total += lax.dot_general(
                    wbuf[dest * 4 + b, k * WPAD : (k + 1) * WPAD, :],
                    attn_ref[:, k * 128 : (k + 1) * 128],
                    NT,
                    preferred_element_type=F32,
                )
            parts.append(total)
        return parts

    def send(d):
        copy = pltpu.make_async_remote_copy(
            src_ref=sbuf.at[d - 1],
            dst_ref=rbuf.at[d - 1],
            send_sem=send_sem.at[d - 1],
            recv_sem=recv_sem.at[d - 1],
            device_id=((gx + d) % nz, gy),
            device_id_type=MESH,
        )
        copy.start()
        return copy

    distances = sorted(range(1, nz), key=lambda d: -min(d, nz - d))
    copies = []
    for n, d in enumerate(distances):
        for b, part in enumerate(partial((gx + d) % nz)):
            sbuf[d - 1, b * WPAD : (b + 1) * WPAD, :] = part.astype(BF16)
        if n == 0:
            pl.semaphore_wait(barrier, nz - 1)
        else:
            copies.append(send(distances[n - 1]))
    parts = partial(gx)
    copies.append(send(distances[-1]))
    bias = jnp.transpose(jnp.broadcast_to(bias_ref[...], (128, bias_ref.shape[1])))
    for copy in copies:
        copy.wait_recv()
    sums = []
    for b in range(4):
        total = parts[b]
        for d in range(1, nz):
            total += rbuf[d - 1, b * WPAD : (b + 1) * WPAD, :].astype(F32)
        sums.append(total[:WCOLS])
    out_ref[...] = (jnp.concatenate(sums, axis=0) + bias).astype(BF16)
    for copy in copies:
        copy.wait_send()


VMEM = pl.BlockSpec(memory_space=pltpu.VMEM)
SMEM = pl.BlockSpec(memory_space=pltpu.SMEM)
ANY = pl.BlockSpec(memory_space=pl.ANY)


def solution(mesh):
    nz = mesh.shape["gx"]
    copies = 76

    def shards(queries, new_kv, kv_cache, cache_seg, cache_slot, token_seg, pad_mask, sink_logits, out_weight, out_bias):
        new2 = new_kv.reshape(TOK, 128)
        kv2 = kv_cache.reshape(SLOTS, 128)
        tseg = token_seg.reshape(1, TOK)
        pad = pad_mask.reshape(1, TOK)
        cache_out, block, own = pl.pallas_call(
            prep_kernel,
            name="prep",
            out_shape=(
                jax.ShapeDtypeStruct((SLOTS, 128), BF16),
                jax.ShapeDtypeStruct((ROWS, 128), BF16),
                jax.ShapeDtypeStruct((8, SLOTS), F32),
            ),
            in_specs=[VMEM] * 7,
            out_specs=(VMEM,) * 3,
            compiler_params=pltpu.CompilerParams(vmem_limit_bytes=VMEM_LIMIT),
        )(new2, kv2, cache_seg.reshape(1, SLOTS), cache_slot.reshape(1, TOK), tseg, pad, out_weight.T)
        gathered = pl.pallas_call(
            lambda *refs: gather_kernel(copies, *refs),
            name="gather",
            out_shape=jax.ShapeDtypeStruct((NBLK, ROWS, 128), BF16),
            in_specs=[VMEM],
            out_specs=ANY,
            scratch_shapes=[
                pltpu.SemaphoreType.DMA,
                pltpu.SemaphoreType.DMA((copies,)),
                pltpu.SemaphoreType.DMA((copies,)),
            ],
            compiler_params=pltpu.CompilerParams(collective_id=0, has_side_effects=True),
        )(block)
        attention = pl.pallas_call(
            attend_kernel,
            name="attend",
            out_shape=jax.ShapeDtypeStruct((TOK, 512), BF16),
            in_specs=[SMEM, SMEM, VMEM, VMEM, VMEM, VMEM, VMEM, ANY],
            out_specs=VMEM,
            scratch_shapes=[
                pltpu.VMEM((NBLK, SLOTS + 80, 128), BF16),
                pltpu.VMEM((NBLK * SLOTS + 640, 128), BF16),
                pltpu.VMEM((NBLK * SLOTS + 640, 128), BF16),
                pltpu.VMEM((8 * TOK, 128), BF16),
                pltpu.VMEM((8 * TOK, 1), F32),
                pltpu.VMEM((8 * TOK, 128), F32),
                pltpu.VMEM((NBLK, 128), jnp.int32),
                pltpu.SMEM((NBLK, 128), jnp.int32),
                pltpu.VMEM((NBLK, 128), jnp.int32),
                pltpu.VMEM((NBLK, 128), jnp.int32),
                pltpu.SemaphoreType.DMA((2,)),
            ],
            compiler_params=pltpu.CompilerParams(vmem_limit_bytes=VMEM_LIMIT),
        )(sink_logits, token_seg, queries, cache_out, own, tseg, pad, gathered)
        projected = pl.pallas_call(
            lambda *refs: project_kernel(nz, *refs),
            name="project",
            out_shape=jax.ShapeDtypeStruct((4 * WCOLS, TOK), BF16),
            in_specs=[VMEM, VMEM, ANY],
            out_specs=VMEM,
            scratch_shapes=[
                pltpu.VMEM((NBLK, WROWS, 128), BF16),
                pltpu.VMEM((nz - 1, WROWS, TOK), BF16),
                pltpu.VMEM((nz - 1, WROWS, TOK), BF16),
                pltpu.SemaphoreType.DMA,
                pltpu.SemaphoreType.DMA((nz - 1,)),
                pltpu.SemaphoreType.DMA((nz - 1,)),
            ],
            compiler_params=pltpu.CompilerParams(
                collective_id=1, has_side_effects=True, vmem_limit_bytes=VMEM_LIMIT
            ),
        )(attention, out_bias.reshape(1, 4 * WCOLS), gathered)
        return projected.T, cache_out.reshape(SLOTS, 1, 128)

    placed = (
        P("gy", "gx"),
        P("gy", "gx", None),
        P("gy", "gx", None),
        P("gy"),
        P("gy"),
        P("gy"),
        P("gy"),
        P("gx"),
        P("gx", "gy"),
        P("gx"),
    )
    return jax.shard_map(
        shards,
        mesh=mesh,
        in_specs=placed,
        out_specs=(P("gy", "gx"), P("gy", "gx", None)),
        check_vma=False,
    )
```

time: 258 us -> 83.5 us (0.32)
  the two profiles are of different devices: /device:TPU:4 before, /device:TPU:15 now
where the time goes in v1:
time: 83.5 us; the launch traced here: 83.3 us
  Pallas kernels  80.5 us (96%)
  local copies, waits for them, and re-layouts  2.1 us (3%)
    pallas_call x1, Pallas kernels, shards(): pl.pallas_call(lambda *refs: gather_kernel(copies, *refs), name='gather',...  29.2 us
    pallas_call x1, Pallas kernels, shards(): pl.pallas_call(lambda *refs: project_kernel(nz, *refs), name='project', o...  28.7 us
    pallas_call x1, Pallas kernels, shards(): pl.pallas_call(attend_kernel, name='attend', out_shape=jax.ShapeDtypeStru...  20.1 us
    pallas_call x1, Pallas kernels, shards(): pl.pallas_call(prep_kernel, name='prep', out_shape=(jax.ShapeDtypeStruct(...  2.48 us

profile of v1, /device:TPU:15, one launch (start us, length us, event | category | flops | bytes accessed | tf_op | source)
XLA Modules:
  0.0 83.3 jit_solution(2190506899836743518)
XLA Ops:
  0.6 2.5 %prep.1 = (bf16[512,128]{1,0:T(8,128)(2,1)}, bf16[912,128]{1,0:T(8,128)(2,1)}, f32[8,512]{1,0:T(8,128)}) custom-call(bf16[128,128]{1,0:T(8,128)(2,1)} %bitcast.13, bf16[512,128]{1,0:T(8,128)(2,1)} %bitcast.11, s32[1,512]{1,0:T(1,128)} %bitcast.16, s32[1,128]{1,0:T(1,128)} %bitcast.19, s32[1,128]{1,0:T(1,128)} %bitcast.14, s32[1,128]{1,0:T(1,128)} %bitcast.17, ...), custom_call_target="tpu_custom_call" | custom-call | tf_op jit(solution)/shard_map/prep/pallas_call | solution.py:393
  3.1 0.0 copy-start
  3.1 29.2 %gather.1.g_ref.refs_2_ = bf16[32,912,128]{2,1,0:T(8,128)(2,1)} custom-call(bf16[912,128]{1,0:T(8,128)(2,1)} %get-tuple-element.7.refs_0_), custom_call_target="tpu_custom_call" | custom-call | tf_op jit(solution)/shard_map/gather/pallas_call | solution.py:405
  32.4 20.1 %attend.1.refs_0_ = bf16[128,512]{1,0:T(8,128)(2,1)} custom-call(f32[8]{0:T(128)} %sink_ref.1, s32[128]{0:T(128)} %tseg_s.1, bf16[128,512]{1,0:T(8,128)(2,1)} %q_ref.1, bf16[512,128]{1,0:T(8,128)(2,1)} %get-tuple-element.5.cache_ref, f32[8,512]{1,0:T(8,128)} %get-tuple-element.6.own_ref, s32[1,128]{1,0:T(1,128)} %bitcast.15, s32[1,128]{1,0:T(1,128)} %bitcast.18, ...), custom_call_target="tpu_custom_call" | custom-call | tf_op jit(solution)/shard_map/attend/pallas_call | solution.py:418
  52.5 0.0 copy-done
  52.5 0.6 reshape.34.refs_1_
  53.1 28.7 %project.1 = bf16[360,128]{1,0:T(8,128)(2,1)} custom-call(bf16[128,512]{1,0:T(8,128)(2,1)} %attend.1.refs_0_, f32[1,360]{1,0:T(1,128)} %reshape.34.refs_1_, bf16[32,912,128]{2,1,0:T(8,128)(2,1)} %gather.1.g_ref.refs_2_), custom_call_target="tpu_custom_call" | custom-call | tf_op jit(solution)/shard_map/project/pallas_call | solution.py:439
  81.7 1.5 %copy.13 = bf16[128,360]{0,1:T(8,128)(2,1)} copy(bf16[128,360]{0,1:T(8,128)(2,1)} %bitcast.9) | data formatting | bytes 184320
Async XLA Ops:
  3.1 49.4 %copy-start = (f32[360]{0:T(512)S(1)}, f32[360]{0:T(512)}, u32[]{:S(2)}) copy-start(f32[360]{0:T(512)} %param.19) | copy-start | bytes 4324

commit v2 on v1

--- a/solution.py
+++ b/solution.py
@@ -315,64 +315,110 @@
         out_ref[:, pair * 128 : (pair + 1) * 128] = (top / bottom * pad_col).astype(BF16)
 
 
-def project_kernel(nz, attn_ref, bias_ref, g_ref, out_ref, wbuf, sbuf, rbuf, load_sem, send_sem, recv_sem):
+def project_kernel(nz, attn_ref, g_ref, out_ref, wbuf, sbuf, rbuf, load_sem, send_sem, recv_sem):
     gx = lax.axis_index("gx")
     gy = lax.axis_index("gy")
-    load = pltpu.make_async_copy(g_ref.at[:, pl.ds(KVROWS, WROWS)], wbuf, load_sem)
-    load.start()
     barrier = pltpu.get_barrier_semaphore()
-    for d in range(1, nz):
+    for d in (1, nz - 1):
         pl.semaphore_signal(barrier, inc=1, device_id=((gx + d) % nz, gy), device_id_type=MESH)
-    load.wait()
-
-    def partial(dest):
-        parts = []
-        for b in range(4):
-            total = jnp.zeros((WPAD, TOK), F32)
-            for k in range(4):
-                total += lax.dot_general(
-                    wbuf[dest * 4 + b, k * WPAD : (k + 1) * WPAD, :],
-                    attn_ref[:, k * 128 : (k + 1) * 128],
-                    NT,
-                    preferred_element_type=F32,
-                )
-            parts.append(total)
-        return parts
-
-    def send(d):
-        copy = pltpu.make_async_remote_copy(
-            src_ref=sbuf.at[d - 1],
-            dst_ref=rbuf.at[d - 1],
-            send_sem=send_sem.at[d - 1],
-            recv_sem=recv_sem.at[d - 1],
-            device_id=((gx + d) % nz, gy),
-            device_id_type=MESH,
-        )
-        copy.start()
-        return copy
-
-    distances = sorted(range(1, nz), key=lambda d: -min(d, nz - d))
-    copies = []
-    for n, d in enumerate(distances):
-        for b, part in enumerate(partial((gx + d) % nz)):
-            sbuf[d - 1, b * WPAD : (b + 1) * WPAD, :] = part.astype(BF16)
-        if n == 0:
-            pl.semaphore_wait(barrier, nz - 1)
+    far = nz // 2
+    offsets = [far]
+    for d in range(far - 1, 0, -1):
+        offsets += [d, -d]
+    offsets.append(0)
+    loads = {}
+    for n, d in enumerate(offsets):
+        blocks = pl.ds(((gx + d + nz) % nz) * 4, 4)
+        loads[d] = pltpu.make_async_copy(g_ref.at[blocks, pl.ds(KVROWS, WROWS)], wbuf.at[blocks], load_sem.at[n])
+        loads[d].start()
+
+    def partial(d):
+        loads[d].wait()
+        dest = (gx + d + nz) % nz
+        total = None
+        for k in (0, 2):
+            sides = []
+            for kk in (k, k + 1):
+                rows = [wbuf[dest * 4 + b, kk * WPAD : (kk + 1) * WPAD, :] for b in range(4)]
+                sides.append(jnp.concatenate(rows, axis=0))
+            part = lax.dot_general(
+                jnp.concatenate(sides, axis=1),
+                attn_ref[:, k * 128 : (k + 2) * 128],
+                NT,
+                preferred_element_type=F32,
+            )
+            total = part if total is None else total + part
+        return total
+
+    def piece(p):
+        return slice(p * WPAD, (p + 1) * WPAD)
+
+    copies = {}
+    waiting = []
+
+    def flush():
+        while waiting:
+            side, step, p = waiting.pop(0)
+            copy = pltpu.make_async_remote_copy(
+                src_ref=sbuf.at[side, step, pl.ds(p * WPAD, WPAD)],
+                dst_ref=rbuf.at[side, step, pl.ds(p * WPAD, WPAD)],
+                send_sem=send_sem.at[side, step, p],
+                recv_sem=recv_sem.at[side, step, p],
+                device_id=((gx + (1 if side == 0 else nz - 1)) % nz, gy),
+                device_id_type=MESH,
+            )
+            copy.start()
+            copies[side, step, p] = copy
+
+    def put(side, step, p, part):
+        value = part[piece(p)]
+        earlier = copies.get((side, step - 1, p))
+        if earlier is not None:
+            earlier.wait_recv()
+            value = value + rbuf[side, step - 1, piece(p), :].astype(F32)
+        sbuf[side, step, piece(p), :] = value.astype(BF16)
+        flush()
+        waiting.append((side, step, p))
+
+    first = [(0, 2), (1, 0), (0, 3), (1, 1)]
+    second = [(0, 0), (1, 2), (0, 1), (1, 3)]
+    part = partial(far)
+    for side, p in second:
+        sbuf[side, 0, piece(p), :] = part[piece(p)].astype(BF16)
+    plus, minus = partial(far - 1), partial(1 - far)
+    pl.semaphore_wait(barrier, 2)
+    waiting += [(side, 0, p) for side, p in second]
+    flush()
+    for step in range(1, far):
+        for side, p in first:
+            put(side, step, p, minus if side else plus)
+        if step == 1:
+            ahead = partial(far - 2)
+            flush()
+            ahead = (ahead, partial(2 - far))
+        for side, p in second:
+            put(side, step, p, minus if side else plus)
+        if step > 1:
+            d = far - step - 1
+            ahead = partial(d)
+            flush()
+            if d > 0:
+                ahead = (ahead, partial(-d))
         else:
-            copies.append(send(distances[n - 1]))
-    parts = partial(gx)
-    copies.append(send(distances[-1]))
-    bias = jnp.transpose(jnp.broadcast_to(bias_ref[...], (128, bias_ref.shape[1])))
-    for copy in copies:
-        copy.wait_recv()
-    sums = []
-    for b in range(4):
-        total = parts[b]
-        for d in range(1, nz):
-            total += rbuf[d - 1, b * WPAD : (b + 1) * WPAD, :].astype(F32)
-        sums.append(total[:WCOLS])
-    out_ref[...] = (jnp.concatenate(sums, axis=0) + bias).astype(BF16)
-    for copy in copies:
+            flush()
+        if step + 1 < far:
+            plus, minus = ahead
+    own = ahead
+    flush()
+    sums = [None] * 4
+    for p in (2, 0, 3, 1):
+        total = own[piece(p)]
+        for side in range(2):
+            copies[side, far - 1, p].wait_recv()
+            total = total + rbuf[side, far - 1, piece(p), :].astype(F32)
+        sums[p] = total[:WCOLS]
+    out_ref[...] = jnp.concatenate(sums, axis=0)
+    for copy in copies.values():
         copy.wait_send()
 
 
@@ -439,22 +485,23 @@
         projected = pl.pallas_call(
             lambda *refs: project_kernel(nz, *refs),
             name="project",
-            out_shape=jax.ShapeDtypeStruct((4 * WCOLS, TOK), BF16),
-            in_specs=[VMEM, VMEM, ANY],
+            out_shape=jax.ShapeDtypeStruct((4 * WCOLS, TOK), F32),
+            in_specs=[VMEM, ANY],
             out_specs=VMEM,
             scratch_shapes=[
                 pltpu.VMEM((NBLK, WROWS, 128), BF16),
-                pltpu.VMEM((nz - 1, WROWS, TOK), BF16),
-                pltpu.VMEM((nz - 1, WROWS, TOK), BF16),
-                pltpu.SemaphoreType.DMA,
-                pltpu.SemaphoreType.DMA((nz - 1,)),
-                pltpu.SemaphoreType.DMA((nz - 1,)),
+                pltpu.VMEM((2, nz // 2, WROWS, TOK), BF16),
+                pltpu.VMEM((2, nz // 2, WROWS, TOK), BF16),
+                pltpu.SemaphoreType.DMA((nz,)),
+                pltpu.SemaphoreType.DMA((2, nz // 2, 4)),
+                pltpu.SemaphoreType.DMA((2, nz // 2, 4)),
             ],
             compiler_params=pltpu.CompilerParams(
                 collective_id=1, has_side_effects=True, vmem_limit_bytes=VMEM_LIMIT
             ),
-        )(attention, out_bias.reshape(1, 4 * WCOLS), gathered)
-        return projected.T, cache_out.reshape(SLOTS, 1, 128)
+        )(attention, gathered)
+        attended = (projected.T + out_bias).astype(BF16)
+        return attended, cache_out.reshape(SLOTS, 1, 128)
 
     placed = (
         P("gy", "gx"),

time: 83.5 us -> 80 us (0.958)
  the two profiles are of different devices: /device:TPU:15 before, /device:TPU:4 now
where the time goes in v2:
time: 80 us; the launch traced here: 79.8 us
  Pallas kernels  77.4 us (97%)
  other arithmetic  1.68 us (2%)
    pallas_call x1, Pallas kernels, shards(): pl.pallas_call(lambda *refs: gather_kernel(copies, *refs), name='gather',...  30.5 us
    pallas_call x1, Pallas kernels, shards(): pl.pallas_call(lambda *refs: project_kernel(nz, *refs), name='project', o...  22.4 us
    pallas_call x1, Pallas kernels, shards(): pl.pallas_call(attend_kernel, name='attend', out_shape=jax.ShapeDtypeStru...  22 us
    pallas_call x1, Pallas kernels, shards(): pl.pallas_call(prep_kernel, name='prep', out_shape=(jax.ShapeDtypeStruct(...  2.48 us
    convert_element_type x1, other arithmetic, shards(): attended = (projected.T + out_bias).astype(BF16)  1.68 us

profile of v2, /device:TPU:4, one launch (start us, length us, event | category | flops | bytes accessed | tf_op | source)
XLA Modules:
  0.0 79.8 jit_solution(3246394562506058626)
XLA Ops:
  0.6 2.5 %prep.1 = (bf16[512,128]{1,0:T(8,128)(2,1)}, bf16[912,128]{1,0:T(8,128)(2,1)}, f32[8,512]{1,0:T(8,128)}) custom-call(bf16[128,128]{1,0:T(8,128)(2,1)} %bitcast.13, bf16[512,128]{1,0:T(8,128)(2,1)} %bitcast.11, s32[1,512]{1,0:T(1,128)} %bitcast.16, s32[1,128]{1,0:T(1,128)} %bitcast.19, s32[1,128]{1,0:T(1,128)} %bitcast.14, s32[1,128]{1,0:T(1,128)} %bitcast.17, ...), custom_call_target="tpu_custom_call" | custom-call | tf_op jit(solution)/shard_map/prep/pallas_call | solution.py:439
  3.1 30.5 %gather.1.g_ref.refs_1_ = bf16[32,912,128]{2,1,0:T(8,128)(2,1)} custom-call(bf16[912,128]{1,0:T(8,128)(2,1)} %get-tuple-element.7.refs_0_), custom_call_target="tpu_custom_call" | custom-call | tf_op jit(solution)/shard_map/gather/pallas_call | solution.py:451
  33.6 0.0 copy-start
  33.6 22.0 %attend.1.refs_0_ = bf16[128,512]{1,0:T(8,128)(2,1)} custom-call(f32[8]{0:T(128)} %sink_ref.1, s32[128]{0:T(128)} %tseg_s.1, bf16[128,512]{1,0:T(8,128)(2,1)} %q_ref.1, bf16[512,128]{1,0:T(8,128)(2,1)} %get-tuple-element.5.cache_ref, f32[8,512]{1,0:T(8,128)} %get-tuple-element.6.own_ref, s32[1,128]{1,0:T(1,128)} %bitcast.15, s32[1,128]{1,0:T(1,128)} %bitcast.18, ...), custom_call_target="tpu_custom_call" | custom-call | tf_op jit(solution)/shard_map/attend/pallas_call | solution.py:464
  55.6 22.4 %project.1 = f32[360,128]{1,0:T(8,128)} custom-call(bf16[128,512]{1,0:T(8,128)(2,1)} %attend.1.refs_0_, bf16[32,912,128]{2,1,0:T(8,128)(2,1)} %gather.1.g_ref.refs_1_), custom_call_target="tpu_custom_call" | custom-call | tf_op jit(solution)/shard_map/project/pallas_call | solution.py:485
  78.1 0.0 copy-done
  78.1 1.7 %fusion = bf16[128,360]{0,1:T(8,128)(2,1)} fusion(f32[360,128]{1,0:T(8,128)} %project.1, f32[360]{0:T(512)S(1)} %copy-done), kind=kLoop, calls=%fused_computation.1 | loop fusion | flops 92160 | bytes 277920 | tf_op jit(solution)/shard_map/convert_element_type | solution.py:503
Async XLA Ops:
  33.6 44.5 %copy-start = (f32[360]{0:T(512)S(1)}, f32[360]{0:T(512)}, u32[]{:S(2)}) copy-start(f32[360]{0:T(512)} %param.19) | copy-start | bytes 4324

commit v3 on v2

--- a/solution.py
+++ b/solution.py
@@ -17,6 +17,7 @@
 WCOLS = 90
 WPAD = 96
 WROWS = 4 * WPAD
+LOADS = 4
 ROWS = KVROWS + WROWS
 PENALTY = -1048576.0
 VMEM_LIMIT = 60 * 1024 * 1024
@@ -85,7 +86,10 @@
     return edges
 
 
-def gather_kernel(copies, blk_ref, out_ref, local_sem, send_sem, recv_sem):
+def gather_kernel(
+    copies, sink_ref, q_ref, cache_ref, own_ref, tseg_ref, blk_ref,
+    out_ref, qa_out, state_out, qa, state, local_sem, save_sem, send_sem, recv_sem,
+):
     gx = lax.axis_index("gx")
     gy = lax.axis_index("gy")
     core = gy % NC
@@ -151,6 +155,30 @@
         d = send(own, lo, hi, second[1], True)
         far[h].append((0, lo, mid, hi, c, d))
         send(own, lo, hi, mate, True)
+    lane = iota((1, 128), 1)
+    low = lane < 64
+    tseg_col = to_column(tseg_ref[...].astype(F32))
+    seg_hot = (tseg_col == (lane - 64).astype(F32)).astype(F32)
+    shift = (iota((128, 128), 0) == iota((128, 128), 1) + 64).astype(BF16)
+    for pair in range(4):
+        two = q_ref[:, pair * 128 : (pair + 1) * 128].astype(F32) * 0.125
+        odd = jnp.dot(two.astype(BF16), shift, preferred_element_type=F32)
+        qa[2 * pair * TOK : (2 * pair + 1) * TOK, :] = jnp.where(low, two, seg_hot).astype(BF16)
+        qa[(2 * pair + 1) * TOK : (2 * pair + 2) * TOK, :] = jnp.where(low, odd, seg_hot).astype(BF16)
+    position = iota((TOK, 1), 0).astype(F32) + 1.0
+    shown = (own_ref[0:1, :] == tseg_col) & (own_ref[1:2, :] <= position)
+    bias = jnp.where(shown, 0.0, PENALTY)
+    kv = cache_ref[...].astype(F32)
+    k_own = jnp.where(low, kv, 0.0).astype(BF16)
+    v_own = jnp.where(low, 1.0, kv).astype(BF16)
+    for h in range(8):
+        rows = slice(h * TOK, (h + 1) * TOK)
+        scores = lax.dot_general(qa[rows, :], k_own, NT, preferred_element_type=F32) + bias
+        peak = jnp.maximum(jnp.max(scores, axis=1, keepdims=True), sink_ref[h])
+        weights = jnp.exp(scores - peak)
+        acc = jnp.dot(weights.astype(BF16), v_own, preferred_element_type=F32)
+        acc = acc + jnp.where(low, jnp.exp(sink_ref[h] - peak), 0.0)
+        state[rows, :] = jnp.where((lane >= 32) & low, peak, acc)
     forward = []
     for h, (lo, mid, hi, first, second, place) in enumerate(halves):
         a, b = near[h]
@@ -181,6 +209,12 @@
 
     for h in range(2):
         relay(h, far[h][0])
+    saves = [
+        pltpu.make_async_copy(qa, qa_out, save_sem.at[0]),
+        pltpu.make_async_copy(state, state_out, save_sem.at[1]),
+    ]
+    for copy in saves:
+        copy.start()
     pieces = []
     for h, (lo, mid, hi, first, second, place) in enumerate(halves):
         fa, fb = forward[h]
@@ -216,43 +250,38 @@
     for copy in started:
         copy.wait_send()
     local.wait()
+    for copy in saves:
+        copy.wait()
     assert used[0] == copies
 
 
 def attend_kernel(
-    sink_ref, tseg_s, q_ref, cache_ref, own_ref, tseg_ref, pad_ref, g_ref,
-    out_ref, buf, ka, va, qa, m_ref, acc_ref, bound_v, bound_s, lo_ref, hi_ref, sems,
+    tseg_s, pad_ref, qa_in, state_in, g_ref,
+    out_ref, buf, heads, ka, va, qa, m_ref, acc_ref, bound_v, bound_s, lo_ref, hi_ref, sems,
 ):
     own_block = lax.axis_index("gy")
-    load = pltpu.make_async_copy(g_ref.at[:, pl.ds(0, KVROWS)], buf.at[:, pl.ds(0, KVROWS)], sems.at[0])
-    load.start()
+    head = pltpu.make_async_copy(g_ref.at[:, pl.ds(SLOTS, META)], heads, sems.at[0])
+    head.start()
+    loads = []
+    for n in range(LOADS):
+        part = pl.ds(n * (NBLK // LOADS), NBLK // LOADS)
+        loads.append(
+            pltpu.make_async_copy(g_ref.at[part, pl.ds(0, SLOTS)], buf.at[part, pl.ds(0, SLOTS)], sems.at[2 + n])
+        )
+        loads[-1].start()
+    restore = [
+        pltpu.make_async_copy(qa_in, qa, sems.at[2 + LOADS]),
+        pltpu.make_async_copy(state_in, acc_ref, sems.at[3 + LOADS]),
+    ]
+    for copy in restore:
+        copy.start()
     lane = iota((1, 128), 1)
     low = lane < 64
-    tseg_col = to_column(tseg_ref[...].astype(F32))
     pad_col = to_column(pad_ref[...].astype(F32))
-    seg_hot = (tseg_col == (lane - 64).astype(F32)).astype(F32)
-    for pair in range(4):
-        two = q_ref[:, pair * 128 : (pair + 1) * 128].astype(F32) * 0.125
-        qa[2 * pair * TOK : (2 * pair + 1) * TOK, :] = jnp.where(low, two, seg_hot).astype(BF16)
-        qa[(2 * pair + 1) * TOK : (2 * pair + 2) * TOK, :] = jnp.where(low, pltpu.roll(two, 64, 1), seg_hot).astype(BF16)
-    position = iota((TOK, 1), 0).astype(F32) + 1.0
-    shown = (own_ref[0:1, :] == tseg_col) & (own_ref[1:2, :] <= position)
-    bias = jnp.where(shown, 0.0, PENALTY)
-    kv = cache_ref[...].astype(F32)
-    k_own = jnp.where(low, kv, 0.0).astype(BF16)
-    v_own = jnp.where(low, 1.0, kv).astype(BF16)
-    for h in range(8):
-        rows = slice(h * TOK, (h + 1) * TOK)
-        scores = lax.dot_general(qa[rows, :], k_own, NT, preferred_element_type=F32) + bias
-        peak = jnp.maximum(jnp.max(scores, axis=1, keepdims=True), sink_ref[h])
-        weights = jnp.exp(scores - peak)
-        acc = jnp.dot(weights.astype(BF16), v_own, preferred_element_type=F32)
-        acc_ref[rows, :] = acc + jnp.where(low, jnp.exp(sink_ref[h] - peak), 0.0)
-        m_ref[rows, :] = peak
-    load.wait()
+    head.wait()
     seg_lo, seg_hi = tseg_s[0], tseg_s[TOK - 1]
     for b in range(NBLK):
-        meta = buf[b, SLOTS:KVROWS, :].astype(F32)
+        meta = heads[b].astype(F32)
         start = meta[0:1] + 256.0 * meta[1:2]
         middle = meta[2:3] + 256.0 * meta[3:4]
         end = meta[4:5] + 256.0 * meta[5:6]
@@ -287,7 +316,14 @@
         lax.fori_loop(0, (length + 63) // 64, piece, 0)
         return off + ((length + 15) // 16) * 16
 
-    total = lax.fori_loop(0, NBLK, pack_block, 0)
+    total = 0
+    for n, load in enumerate(loads):
+        load.wait()
+        total = lax.fori_loop(n * (NBLK // LOADS), (n + 1) * (NBLK // LOADS), pack_block, total)
+    for copy in restore:
+        copy.wait()
+    m_ref[...] = acc_ref[:, 32:33]
+    acc_ref[...] = jnp.where((lane >= 32) & low, pltpu.roll(acc_ref[...], 32, 1), acc_ref[...])
     tail = pl.multiple_of(total, 16)
     ka[pl.ds(tail, 512), :] = jnp.broadcast_to(jnp.where(low, 0.0, PENALTY), (512, 128)).astype(BF16)
     va[pl.ds(tail, 512), :] = jnp.broadcast_to(jnp.where(low, 1.0, 0.0), (512, 128)).astype(BF16)
@@ -448,27 +484,37 @@
             out_specs=(VMEM,) * 3,
             compiler_params=pltpu.CompilerParams(vmem_limit_bytes=VMEM_LIMIT),
         )(new2, kv2, cache_seg.reshape(1, SLOTS), cache_slot.reshape(1, TOK), tseg, pad, out_weight.T)
-        gathered = pl.pallas_call(
+        gathered, qa, state = pl.pallas_call(
             lambda *refs: gather_kernel(copies, *refs),
             name="gather",
-            out_shape=jax.ShapeDtypeStruct((NBLK, ROWS, 128), BF16),
-            in_specs=[VMEM],
-            out_specs=ANY,
+            out_shape=(
+                jax.ShapeDtypeStruct((NBLK, ROWS, 128), BF16),
+                jax.ShapeDtypeStruct((8 * TOK, 128), BF16),
+                jax.ShapeDtypeStruct((8 * TOK, 128), F32),
+            ),
+            in_specs=[SMEM, VMEM, VMEM, VMEM, VMEM, VMEM],
+            out_specs=(ANY,) * 3,
             scratch_shapes=[
+                pltpu.VMEM((8 * TOK, 128), BF16),
+                pltpu.VMEM((8 * TOK, 128), F32),
                 pltpu.SemaphoreType.DMA,
+                pltpu.SemaphoreType.DMA((2,)),
                 pltpu.SemaphoreType.DMA((copies,)),
                 pltpu.SemaphoreType.DMA((copies,)),
             ],
-            compiler_params=pltpu.CompilerParams(collective_id=0, has_side_effects=True),
-        )(block)
+            compiler_params=pltpu.CompilerParams(
+                collective_id=0, has_side_effects=True, vmem_limit_bytes=VMEM_LIMIT
+            ),
+        )(sink_logits, queries, cache_out, own, tseg, block)
         attention = pl.pallas_call(
             attend_kernel,
             name="attend",
             out_shape=jax.ShapeDtypeStruct((TOK, 512), BF16),
-            in_specs=[SMEM, SMEM, VMEM, VMEM, VMEM, VMEM, VMEM, ANY],
+            in_specs=[SMEM, VMEM, ANY, ANY, ANY],
             out_specs=VMEM,
             scratch_shapes=[
                 pltpu.VMEM((NBLK, SLOTS + 80, 128), BF16),
+                pltpu.VMEM((NBLK, META, 128), BF16),
                 pltpu.VMEM((NBLK * SLOTS + 640, 128), BF16),
                 pltpu.VMEM((NBLK * SLOTS + 640, 128), BF16),
                 pltpu.VMEM((8 * TOK, 128), BF16),
@@ -478,10 +524,10 @@
                 pltpu.SMEM((NBLK, 128), jnp.int32),
                 pltpu.VMEM((NBLK, 128), jnp.int32),
                 pltpu.VMEM((NBLK, 128), jnp.int32),
-                pltpu.SemaphoreType.DMA((2,)),
+                pltpu.SemaphoreType.DMA((4 + LOADS,)),
             ],
             compiler_params=pltpu.CompilerParams(vmem_limit_bytes=VMEM_LIMIT),
-        )(sink_logits, token_seg, queries, cache_out, own, tseg, pad, gathered)
+        )(token_seg, pad, qa, state, gathered)
         projected = pl.pallas_call(
             lambda *refs: project_kernel(nz, *refs),
             name="project",

time: 80 us -> 76.2 us (0.953)
  the two profiles are of different devices: /device:TPU:4 before, /device:TPU:22 now
where the time goes in v3:
time: 76.2 us; the launch traced here: 76 us
  Pallas kernels  73.6 us (97%)
  other arithmetic  1.68 us (2%)
    pallas_call x1, Pallas kernels, shards(): pl.pallas_call(lambda *refs: gather_kernel(copies, *refs), name='gather',...  28 us
    pallas_call x1, Pallas kernels, shards(): pl.pallas_call(lambda *refs: project_kernel(nz, *refs), name='project', o...  22.4 us
    pallas_call x1, Pallas kernels, shards(): pl.pallas_call(attend_kernel, name='attend', out_shape=jax.ShapeDtypeStru...  20.7 us
    pallas_call x1, Pallas kernels, shards(): pl.pallas_call(prep_kernel, name='prep', out_shape=(jax.ShapeDtypeStruct(...  2.52 us
    convert_element_type x1, other arithmetic, shards(): attended = (projected.T + out_bias).astype(BF16)  1.68 us

profile of v3, /device:TPU:22, one launch (start us, length us, event | category | flops | bytes accessed | tf_op | source)
XLA Modules:
  0.0 76.0 jit_solution(9501697132637548368)
XLA Ops:
  0.6 2.5 %prep.1 = (bf16[512,128]{1,0:T(8,128)(2,1)}, bf16[912,128]{1,0:T(8,128)(2,1)}, f32[8,512]{1,0:T(8,128)}) custom-call(bf16[128,128]{1,0:T(8,128)(2,1)} %bitcast.13, bf16[512,128]{1,0:T(8,128)(2,1)} %bitcast.10, s32[1,512]{1,0:T(1,128)} %bitcast.16, s32[1,128]{1,0:T(1,128)} %bitcast.19, s32[1,128]{1,0:T(1,128)} %bitcast.14, s32[1,128]{1,0:T(1,128)} %bitcast.17, ...), custom_call_target="tpu_custom_call" | custom-call | tf_op jit(solution)/shard_map/prep/pallas_call | solution.py:475
  3.1 28.0 %gather.1 = (bf16[32,912,128]{2,1,0:T(8,128)(2,1)}, bf16[1024,128]{1,0:T(8,128)(2,1)}, f32[1024,128]{1,0:T(8,128)}) custom-call(f32[8]{0:T(128)} %refs_0_.1, bf16[128,512]{1,0:T(8,128)(2,1)} %refs_1_.1, bf16[512,128]{1,0:T(8,128)(2,1)} %get-tuple-element.8.refs_2_, f32[8,512]{1,0:T(8,128)} %get-tuple-element.9.refs_3_, s32[1,128]{1,0:T(1,128)} %bitcast.15, ...), custom_call_target="tpu_custom_call" | custom-call | tf_op jit(solution)/shard_map/gather/pallas_call | solution.py:487
  31.2 0.0 copy-start
  31.2 20.7 %attend.1.refs_0_ = bf16[128,512]{1,0:T(8,128)(2,1)} custom-call(s32[128]{0:T(128)} %tseg_s.1, s32[1,128]{1,0:T(1,128)} %bitcast.18, bf16[1024,128]{1,0:T(8,128)(2,1)} %get-tuple-element.11.qa_in, f32[1024,128]{1,0:T(8,128)} %get-tuple-element.12.state_in, bf16[32,912,128]{2,1,0:T(8,128)(2,1)} %get-tuple-element.13.g_ref.refs_1_), custom_call_target="tpu_custom_call" | custom-call | tf_op jit(solution)/shard_map/attend/pallas_call | solution.py:509
  51.9 22.4 %project.1 = f32[360,128]{1,0:T(8,128)} custom-call(bf16[128,512]{1,0:T(8,128)(2,1)} %attend.1.refs_0_, bf16[32,912,128]{2,1,0:T(8,128)(2,1)} %get-tuple-element.13.g_ref.refs_1_), custom_call_target="tpu_custom_call" | custom-call | tf_op jit(solution)/shard_map/project/pallas_call | solution.py:531
  74.3 0.0 copy-done
  74.3 1.7 %fusion = bf16[128,360]{0,1:T(8,128)(2,1)} fusion(f32[360,128]{1,0:T(8,128)} %project.1, f32[360]{0:T(512)S(1)} %copy-done), kind=kLoop, calls=%fused_computation.1 | loop fusion | flops 92160 | bytes 277920 | tf_op jit(solution)/shard_map/convert_element_type | solution.py:549
Async XLA Ops:
  31.2 43.1 %copy-start = (f32[360]{0:T(512)S(1)}, f32[360]{0:T(512)}, u32[]{:S(2)}) copy-start(f32[360]{0:T(512)} %param.19) | copy-start | bytes 4324

commit v4 on v3

--- a/solution.py
+++ b/solution.py
@@ -18,6 +18,8 @@
 WPAD = 96
 WROWS = 4 * WPAD
 LOADS = 4
+GROUP = 128
+CHUNK = 256
 ROWS = KVROWS + WROWS
 PENALTY = -1048576.0
 VMEM_LIMIT = 60 * 1024 * 1024
@@ -322,27 +324,34 @@
         total = lax.fori_loop(n * (NBLK // LOADS), (n + 1) * (NBLK // LOADS), pack_block, total)
     for copy in restore:
         copy.wait()
-    m_ref[...] = acc_ref[:, 32:33]
+    m_ref[...] = jnp.broadcast_to(acc_ref[:, 32:33], (8 * TOK, 128))
     acc_ref[...] = jnp.where((lane >= 32) & low, pltpu.roll(acc_ref[...], 32, 1), acc_ref[...])
     tail = pl.multiple_of(total, 16)
-    ka[pl.ds(tail, 512), :] = jnp.broadcast_to(jnp.where(low, 0.0, PENALTY), (512, 128)).astype(BF16)
-    va[pl.ds(tail, 512), :] = jnp.broadcast_to(jnp.where(low, 1.0, 0.0), (512, 128)).astype(BF16)
+    ka[pl.ds(tail, CHUNK), :] = jnp.broadcast_to(jnp.where(low, 0.0, PENALTY), (CHUNK, 128)).astype(BF16)
+    va[pl.ds(tail, CHUNK), :] = jnp.broadcast_to(jnp.where(low, 1.0, 0.0), (CHUNK, 128)).astype(BF16)
 
     def chunk(i, carry):
-        at = pl.multiple_of(i * 512, 512)
-        keys, values = ka[pl.ds(at, 512), :], va[pl.ds(at, 512), :]
-        for r in range(4):
-            rows = slice(r * 256, (r + 1) * 256)
-            scores = lax.dot_general(qa[rows, :], keys, NT, preferred_element_type=F32)
+        at = pl.multiple_of(i * CHUNK, CHUNK)
+        keys, values = ka[pl.ds(at, CHUNK), :], va[pl.ds(at, CHUNK), :]
+
+        def score(r):
+            return lax.dot_general(qa[r * GROUP : (r + 1) * GROUP, :], keys, NT, preferred_element_type=F32)
+
+        upcoming = score(0)
+        for r in range(8 * TOK // GROUP):
+            rows = slice(r * GROUP, (r + 1) * GROUP)
+            scores = upcoming
+            if (r + 1) * GROUP < 8 * TOK:
+                upcoming = score(r + 1)
             old = m_ref[rows, :]
             peak = jnp.maximum(old, jnp.max(scores, axis=1, keepdims=True))
-            weights = jnp.exp(scores - peak)
-            acc = jnp.dot(weights.astype(BF16), values, preferred_element_type=F32)
+            weights = [jnp.exp(scores[:, c : c + 128] - peak).astype(BF16) for c in range(0, CHUNK, 128)]
+            acc = jnp.dot(jnp.concatenate(weights, axis=1), values, preferred_element_type=F32)
             acc_ref[rows, :] = acc_ref[rows, :] * jnp.exp(old - peak) + acc
             m_ref[rows, :] = peak
         return carry
 
-    lax.fori_loop(0, (total + 511) // 512, chunk, 0)
+    lax.fori_loop(0, (total + CHUNK - 1) // CHUNK, chunk, 0)
     for pair in range(4):
         even = acc_ref[2 * pair * TOK : (2 * pair + 1) * TOK, :]
         odd = acc_ref[(2 * pair + 1) * TOK : (2 * pair + 2) * TOK, :]
@@ -515,10 +524,10 @@
             scratch_shapes=[
                 pltpu.VMEM((NBLK, SLOTS + 80, 128), BF16),
                 pltpu.VMEM((NBLK, META, 128), BF16),
-                pltpu.VMEM((NBLK * SLOTS + 640, 128), BF16),
-                pltpu.VMEM((NBLK * SLOTS + 640, 128), BF16),
+                pltpu.VMEM((NBLK * SLOTS + CHUNK + 128, 128), BF16),
+                pltpu.VMEM((NBLK * SLOTS + CHUNK + 128, 128), BF16),
                 pltpu.VMEM((8 * TOK, 128), BF16),
-                pltpu.VMEM((8 * TOK, 1), F32),
+                pltpu.VMEM((8 * TOK, 128), F32),
                 pltpu.VMEM((8 * TOK, 128), F32),
                 pltpu.VMEM((NBLK, 128), jnp.int32),
                 pltpu.SMEM((NBLK, 128), jnp.int32),

time: 76.2 us -> 72.5 us (0.951)
  the two profiles are of different devices: /device:TPU:22 before, /device:TPU:4 now
where the time goes in v4:
time: 72.5 us; the launch traced here: 72.3 us
  Pallas kernels  69.9 us (96%)
  other arithmetic  1.68 us (2%)
    pallas_call x1, Pallas kernels, shards(): pl.pallas_call(lambda *refs: gather_kernel(copies, *refs), name='gather',...  30.7 us
    pallas_call x1, Pallas kernels, shards(): pl.pallas_call(lambda *refs: project_kernel(nz, *refs), name='project', o...  22.7 us
    pallas_call x1, Pallas kernels, shards(): pl.pallas_call(attend_kernel, name='attend', out_shape=jax.ShapeDtypeStru...  14 us
    pallas_call x1, Pallas kernels, shards(): pl.pallas_call(prep_kernel, name='prep', out_shape=(jax.ShapeDtypeStruct(...  2.51 us
    convert_element_type x1, other arithmetic, shards(): attended = (projected.T + out_bias).astype(BF16)  1.68 us

profile of v4, /device:TPU:4, one launch (start us, length us, event | category | flops | bytes accessed | tf_op | source)
XLA Modules:
  0.0 72.3 jit_solution(12501478541699731570)
XLA Ops:
  0.6 2.5 %prep.1 = (bf16[512,128]{1,0:T(8,128)(2,1)}, bf16[912,128]{1,0:T(8,128)(2,1)}, f32[8,512]{1,0:T(8,128)}) custom-call(bf16[128,128]{1,0:T(8,128)(2,1)} %bitcast.13, bf16[512,128]{1,0:T(8,128)(2,1)} %bitcast.10, s32[1,512]{1,0:T(1,128)} %bitcast.16, s32[1,128]{1,0:T(1,128)} %bitcast.19, s32[1,128]{1,0:T(1,128)} %bitcast.14, s32[1,128]{1,0:T(1,128)} %bitcast.17, ...), custom_call_target="tpu_custom_call" | custom-call | tf_op jit(solution)/shard_map/prep/pallas_call | solution.py:484
  3.1 30.7 %gather.1 = (bf16[32,912,128]{2,1,0:T(8,128)(2,1)}, bf16[1024,128]{1,0:T(8,128)(2,1)}, f32[1024,128]{1,0:T(8,128)}) custom-call(f32[8]{0:T(128)} %refs_0_.1, bf16[128,512]{1,0:T(8,128)(2,1)} %refs_1_.1, bf16[512,128]{1,0:T(8,128)(2,1)} %get-tuple-element.8.refs_2_, f32[8,512]{1,0:T(8,128)} %get-tuple-element.9.refs_3_, s32[1,128]{1,0:T(1,128)} %bitcast.15, ...), custom_call_target="tpu_custom_call" | custom-call | tf_op jit(solution)/shard_map/gather/pallas_call | solution.py:496
  33.9 0.0 copy-start
  33.9 14.0 %attend.1.refs_0_ = bf16[128,512]{1,0:T(8,128)(2,1)} custom-call(s32[128]{0:T(128)} %tseg_s.1, s32[1,128]{1,0:T(1,128)} %bitcast.18, bf16[1024,128]{1,0:T(8,128)(2,1)} %get-tuple-element.11.qa_in, f32[1024,128]{1,0:T(8,128)} %get-tuple-element.12.state_in, bf16[32,912,128]{2,1,0:T(8,128)(2,1)} %get-tuple-element.13.g_ref.refs_1_), custom_call_target="tpu_custom_call" | custom-call | tf_op jit(solution)/shard_map/attend/pallas_call | solution.py:518
  47.9 22.7 %project.1 = f32[360,128]{1,0:T(8,128)} custom-call(bf16[128,512]{1,0:T(8,128)(2,1)} %attend.1.refs_0_, bf16[32,912,128]{2,1,0:T(8,128)(2,1)} %get-tuple-element.13.g_ref.refs_1_), custom_call_target="tpu_custom_call" | custom-call | tf_op jit(solution)/shard_map/project/pallas_call | solution.py:540
  70.6 0.0 copy-done
  70.6 1.7 %fusion = bf16[128,360]{0,1:T(8,128)(2,1)} fusion(f32[360,128]{1,0:T(8,128)} %project.1, f32[360]{0:T(512)S(1)} %copy-done), kind=kLoop, calls=%fused_computation.1 | loop fusion | flops 92160 | bytes 277920 | tf_op jit(solution)/shard_map/convert_element_type | solution.py:558
Async XLA Ops:
  33.9 36.7 %copy-start = (f32[360]{0:T(512)S(1)}, f32[360]{0:T(512)}, u32[]{:S(2)}) copy-start(f32[360]{0:T(512)} %param.19) | copy-start | bytes 4324
